TPU v7x, 32 devices: a whole 2x2x4 slice. The times are simulated.
32 devices in a mesh: row: 4 (over z), col: 8 (over y, x, core).
Axes of the slice: x: 2, y: 2, z: 4, core: 2. Of those that a mesh axis runs over, the one named last changes fastest.
Arguments:
- normal_matrix: float32 [14336, 14336], P(('row', 'col')), may hold values from -90 to 90, as said below
- new_index: int32 [14336], replicated, may hold values from 0 to 14335, each once
- check_vectors: float32 [14336, 1024], P('col'), may hold values from -0.046875 to 0.046875
Outputs:
- tile_layout: float32 [14336, 14336], P('row', 'col')
- check_product: float32 [14336, 1024], P(('row', 'col'))
Inputs may be any that keep to these rules, and one draw needn't show every extreme that they name: normal_matrix is symmetric. new_index[a] is the new index of parameter a; every index 0 to 14335 appears once.
All inputs are finite; a program needn't handle non-finite values.
Results may differ from a plain program's by a relative error of at most 0.000082.
Values sent between devices are 32-bit elements; how exact they have to be, the bound alone decides.
A program may use at most 192 MiB of HBM per device.

v0:
```python
import jax
import jax.numpy as jnp
from jax import lax
from jax.sharding import PartitionSpec as P

TILE = 128


def new_of_packed(places, groups, stride, tile_size):
    holder = places // stride
    within = places % stride
    return (within // tile_size * groups + holder) * tile_size + within % tile_size


def shards(normal_matrix, new_index, check_vectors):
    row_count = lax.axis_size("row")
    col_count = lax.axis_size("col")
    devices = row_count * col_count
    unknowns = new_index.shape[0]
    slab_rows = normal_matrix.shape[0]
    share = unknowns // devices
    places = jnp.arange(unknowns, dtype=jnp.int32)
    old_of_new = jnp.zeros((unknowns,), jnp.int32).at[new_index].set(places)
    row_pick = old_of_new[new_of_packed(places, row_count, unknowns // row_count, TILE)]
    col_pick = old_of_new[new_of_packed(places, col_count, unknowns // col_count, TILE)]
    gathered = jnp.take(normal_matrix.T, row_pick, axis=0)
    grouped = gathered.reshape(devices, share, slab_rows).transpose(0, 2, 1)
    outgoing = grouped.reshape(devices * slab_rows, share)
    arrived = lax.all_to_all(outgoing, ("row", "col"), split_axis=0, concat_axis=0, tiled=True)
    chosen = jnp.take(arrived, col_pick, axis=0)
    moved = lax.all_to_all(chosen, "col", split_axis=0, concat_axis=1, tiled=True)
    tile_layout = moved.T
    check_product = lax.psum_scatter(
        jnp.dot(
            tile_layout,
            check_vectors,
            precision=lax.Precision.HIGHEST,
            preferred_element_type=jnp.float32,
        ),
        "col",
        scatter_dimension=0,
        tiled=True,
    )
    return (tile_layout, check_product)


def solution(mesh):
    return jax.shard_map(
        shards,
        mesh=mesh,
        in_specs=(P(("row", "col"), None), P(), P("col", None)),
        out_specs=(P("row", "col"), P(("row", "col"), None)),
        check_vma=False,
    )
```

profile of v0, /device:TPU:0, one launch (start us, length us, event | category | flops | bytes accessed | tf_op | source)
XLA Modules:
  0.0 1578.4 jit_solution(10334627582451271327)
XLA Ops:
  7.2 0.7 compare_select_fusion.1
  7.9 0.8 compare_select_fusion.4
  8.7 52.9 %scatter_custom_fusion = s32[14336]{0:T(1024)S(1)} fusion(s32[14336]{0:T(1024)S(1)} %compare_select_fusion.4, s32[14336]{0:T(1024)S(1)} %iota.11, s32[]{:T(128)} %constant.71.clone.1), kind=kCustom, calls=%fused_computation.43 | custom fusion | bytes 57348 | tf_op jit(solution)/shard_map/scatter | solution.py:23
  61.6 79.3 %gather_fusion = s32[14336]{0:T(1024)S(1)} fusion(s32[14336]{0:T(1024)S(1)} %scatter_custom_fusion, s32[14336]{0:T(1024)S(1)} %broadcast_clamp_fusion), kind=kCustom, calls=%fused_computation.2 | custom fusion | bytes 172032 | tf_op jit(solution)/shard_map/gather | solution.py:24
  141.0 28.0 %copy.11 = f32[448,14336]{0,1:T(8,128)} copy(f32[448,14336]{1,0:T(8,128)} %param.5) | data formatting | bytes 51380224 | tf_op args[0]
  169.0 69.9 %gather_fusion.2 = f32[14336,448]{1,0:T(8,128)} fusion(f32[14336,448]{1,0:T(8,128)} %bitcast.17, s32[14336]{0:T(1024)S(1)} %fusion.6), kind=kCustom, calls=%fused_computation.clone | custom fusion | bytes 51437568 | tf_op jit(solution)/shard_map/jit(_take)/gather | solution.py:26
  238.8 21.4 %broadcast_select_fusion.1 = f32[14336,448]{1,0:T(8,128)} fusion(f32[14336,448]{1,0:T(8,128)} %gather_fusion.2, pred[14336]{0:T(1024)(128)(4,1)S(1)} %compare_and_fusion.1), kind=kLoop, calls=%fused_computation.6 | loop fusion | flops 6422528 | bytes 51394560 | tf_op jit(solution)/shard_map/jit(_take)/select_n | solution.py:26
  260.2 7.4 all-to-all-start
  267.7 0.0 reduce-scatter.2.cloned.1.call-start
  267.7 0.7 compare_select_fusion
  268.5 79.3 %gather_fusion.1 = s32[14336]{0:T(1024)S(1)} fusion(s32[14336]{0:T(1024)S(1)} %scatter_custom_fusion, s32[14336]{0:T(1024)S(1)} %broadcast_clamp_fusion.1), kind=kCustom, calls=%fused_computation.3 | custom fusion | bytes 172032 | tf_op jit(solution)/shard_map/gather | solution.py:25
  347.8 574.5 %all-to-all-done = f32[32,448,448]{1,2,0:T(8,128)} async-done(((f32[32,448,448]{1,2,0:T(8,128)}), f32[32,448,448]{1,2,0:T(8,128)}, u32[]{:S(2)}, u32[]{:S(2)}) %all-to-all-start) | async-done | bytes 25690144 | tf_op jit(solution)/shard_map/all_to_all | solution.py:29
  922.4 31.1 %copy.12 = f32[32,448,448]{2,1,0:T(8,128)} copy(f32[32,448,448]{1,2,0:T(8,128)} %all-to-all-done) | data formatting | bytes 51380224 | tf_op jit(solution)/shard_map/all_to_all | solution.py:29
  953.5 70.0 %gather_fusion.3 = f32[14336,448]{1,0:T(8,128)} fusion(f32[14336,448]{1,0:T(8,128)} %bitcast.16, s32[14336]{0:T(1024)S(1)} %fusion.7), kind=kCustom, calls=%fused_computation.1.clone | custom fusion | bytes 51437568 | tf_op jit(solution)/shard_map/jit(_take)/gather | solution.py:30
  1023.5 21.4 %broadcast_select_fusion = f32[14336,448]{1,0:T(8,128)} fusion(f32[14336,448]{1,0:T(8,128)} %gather_fusion.3, pred[14336]{0:T(1024)(128)(4,1)S(1)} %compare_and_fusion), kind=kLoop, calls=%fused_computation.5 | loop fusion | flops 6422528 | bytes 51394560 | tf_op jit(solution)/shard_map/jit(_take)/select_n | solution.py:30
  1044.9 26.7 %copy.13 = f32[8,1792,448]{1,2,0:T(8,128)} copy(f32[8,1792,448]{2,1,0:T(8,128)} %bitcast.19) | data formatting | bytes 51380224 | tf_op jit(solution)/shard_map/all_to_all | solution.py:31
  1071.6 289.0 %all_to_all.28 = f32[8,1792,448]{1,2,0:T(8,128)} all-to-all(f32[8,1792,448]{1,2,0:T(8,128)} %copy.13), channel_id=1, replica_groups=mesh['row'=4,'col'=8] {'col'}, dimensions={0} | all-to-all | bytes 51380224 | tf_op jit(solution)/shard_map/all_to_all | solution.py:31
  1360.6 92.6 %fusion.10 = f32[3584,1024]{1,0:T(8,128)} fusion(f32[1792,3584]{0,1:T(8,128)} %bitcast.20, f32[1792,1024]{1,0:T(8,128)} %param.7), kind=kOutput, calls=%fused_computation.45 | convolution fusion | flops 78920024064 | bytes 47710208 | tf_op jit(solution)/shard_map/dot_general | solution.py:34
  1453.2 0.0 reduce-scatter.2.cloned.1.call-update
  1453.2 101.1 %reduce-scatter.2.cloned.1.call-done = f32[448,1024]{1,0:T(8,128)} async-done(((f32[3584,1024]{1,0:T(8,128)}), f32[448,1024]{1,0:T(8,128)}) %reduce-scatter.2.cloned.1.call-update) | async-done | bytes 1835024 | tf_op jit(solution)/shard_map/reduce_scatter | solution.py:33
  1554.3 17.3 %copy.15 = f32[3584,1792]{1,0:T(8,128)} copy(f32[3584,1792]{1,0:T(8,128)} %bitcast.21) | data formatting | bytes 51380224
  (7 shorter events, 0.1 us)
Async XLA Ops:
  260.2 662.1 %all-to-all-start = ((f32[32,448,448]{1,2,0:T(8,128)}), f32[32,448,448]{1,2,0:T(8,128)}, u32[]{:S(2)}, u32[]{:S(2)}) async-start(f32[32,448,448]{1,2,0:T(8,128)} %bitcast.18), calls=%async_computation | async-start | bytes 58720256 | tf_op jit(solution)/shard_map/all_to_all | solution.py:29
  267.7 1286.6 %reduce-scatter.2.cloned.1.call-start = ((), (), s32[]{:S(2)}) async-start(), calls=%async_computation.3 | async-start | bytes 16515072 | tf_op jit(solution)/shard_map/reduce_scatter | solution.py:33
Sparse Core Ops, SparseCore 0:
  1453.4 100.9 reduce-scatter.1
where the time goes:
time: 1580 us
  waiting for transfers between devices  676 us (43%)
  local copies, waits for them, and re-layouts  454 us (29%)
  blocking collectives  289 us (18%)
  matrix products  92.6 us (6%)
  other arithmetic  45.2 us (3%)
    all_to_all x1, waiting for transfers between devices, shards(): lax.all_to_all(outgoing, ('row', 'col'), split_axis=0, concat_axis=0, til...  575 us
    all_to_all x1, blocking collectives, shards(): lax.all_to_all(chosen, 'col', split_axis=0, concat_axis=1, tiled=True)  289 us
    reduce_scatter x1, waiting for transfers between devices, shards(): lax.psum_scatter(jnp.dot(tile_layout, check_vectors, precision=lax.Precis...  101 us
    dot_general x1, matrix products, shards(): jnp.dot(tile_layout, check_vectors, precision=lax.Precision.HIGHEST, pref...  92.6 us
    gather x1, local copies, waits for them, and re-layouts, shards(): old_of_new[new_of_packed(places, row_count, unknowns // row_count, TILE)]  79.3 us
    gather x1, local copies, waits for them, and re-layouts, shards(): old_of_new[new_of_packed(places, col_count, unknowns // col_count, TILE)]  79.3 us
    gather x1, local copies, waits for them, and re-layouts, shards(): chosen = jnp.take(arrived, col_pick, axis=0)  70 us
    gather x1, local copies, waits for them, and re-layouts, shards(): gathered = jnp.take(normal_matrix.T, row_pick, axis=0)  69.9 us
  transfers between devices with their start and end apart: 2, of which 2 were waited for; matrix products, arithmetic and copies ran while one was open for 5% of the time, Pallas kernels for 0%

commit v1 on v0

v1 whole, which is shorter than its diff:
```python
import jax
import jax.numpy as jnp
from jax import lax
from jax.sharding import PartitionSpec as P

TILE = 128
WIDTHS = 4


def inverse_of(new_index):
    unknowns = new_index.shape[0]
    tiles = unknowns // TILE
    places = jnp.arange(unknowns, dtype=jnp.int32)
    high = (new_index // TILE)[None, :] == jnp.arange(tiles, dtype=jnp.int32)[:, None]
    low = (new_index % TILE)[:, None] == jnp.arange(TILE, dtype=jnp.int32)[None, :]
    digits = jnp.concatenate(
        [
            jnp.where(low, (places // TILE)[:, None], 0).astype(jnp.bfloat16),
            jnp.where(low, (places % TILE)[:, None], 0).astype(jnp.bfloat16),
        ],
        axis=1,
    )
    found = jnp.dot(high.astype(jnp.bfloat16), digits, preferred_element_type=jnp.float32)
    found = found.astype(jnp.int32)
    return found[:, :TILE] * TILE + found[:, TILE:]


def cyclic(old_of_new, groups):
    tiles = old_of_new.shape[0]
    return old_of_new.reshape(tiles // groups, groups, TILE).transpose(1, 0, 2).reshape(-1)


def rows_of(matrix, picks):
    return matrix.at[picks].get(mode="promise_in_bounds", unique_indices=True)


def cuts_of(share):
    step = -(-share // WIDTHS)
    step = -(-step // 8) * 8
    return [(at, min(step, share - at)) for at in range(0, share, step)]


def shards(normal_matrix, new_index, check_vectors):
    row_count = lax.axis_size("row")
    col_count = lax.axis_size("col")
    devices = row_count * col_count
    unknowns = new_index.shape[0]
    slab_rows = normal_matrix.shape[0]
    share = unknowns // devices
    old_of_new = inverse_of(new_index)
    row_pick = cyclic(old_of_new, row_count).reshape(devices, share)
    col_pick = cyclic(old_of_new, col_count)
    turned = normal_matrix.T
    blocks, products = [], []
    for at, width in cuts_of(share):
        picks = row_pick[:, at : at + width].reshape(-1)
        outgoing = rows_of(turned, picks).reshape(devices, width, slab_rows)
        arrived = lax.all_to_all(outgoing, ("row", "col"), split_axis=0, concat_axis=0, tiled=True)
        by_old = arrived.transpose(0, 2, 1).reshape(unknowns, width)
        chosen = rows_of(by_old, col_pick).reshape(col_count, unknowns // col_count, width)
        moved = lax.all_to_all(chosen.transpose(0, 2, 1), "col", split_axis=0, concat_axis=0, tiled=True)
        blocks.append(moved)
        partial = jnp.dot(
            moved.reshape(col_count * width, -1),
            check_vectors,
            precision=lax.Precision.HIGH,
            preferred_element_type=jnp.float32,
        )
        products.append(lax.psum_scatter(partial, "col", scatter_dimension=0, tiled=True))
    tile_layout = jnp.concatenate(blocks, axis=1).reshape(col_count * share, -1)
    return (tile_layout, jnp.concatenate(products, axis=0))


def solution(mesh):
    return jax.shard_map(
        shards,
        mesh=mesh,
        in_specs=(P(("row", "col"), None), P(), P("col", None)),
        out_specs=(P("row", "col"), P(("row", "col"), None)),
        check_vma=False,
    )
```

time: 1580 us -> 1160 us (0.73)
  blocking collectives: 289 us -> 0 us
  local copies, waits for them, and re-layouts: 454 us -> 385 us
  waiting for transfers between devices: 676 us -> 622 us
  starting transfers between devices: 7.48 us -> 38 us
  matrix products: 92.6 us -> 63.6 us
    all_to_all x1 -> x0, blocking collectives: 289 us -> none  [shards(): lax.all_to_all(chosen, 'col', split_axis=0, concat_axis=1, tiled=True)]
    reduce_scatter x1 -> x4, waiting for transfers between devices: 101 us -> 25.9 us  [shards(): lax.psum_scatter(partial, 'col', scatter_dimension=0, tiled=True)]
    all_to_all x0 -> x4, waiting for transfers between devices: none -> 75 us  [shards(): lax.all_to_all(chosen.transpose(0, 2, 1), 'col', split_axis=0, concat_axi...]
    all_to_all x2 -> x0, local copies, waits for them, and re-layouts: 57.8 us -> none  [the longest x1 31.1 us: shards(): lax.all_to_all(outgoing, ('row', 'col'), split_axis=0, concat_axis=0, til...]
    all_to_all x1 -> x4, waiting for transfers between devices: 575 us -> 521 us  [shards(): lax.all_to_all(outgoing, ('row', 'col'), split_axis=0, concat_axis=0, til...]
    scatter x1 -> x0, local copies, waits for them, and re-layouts: 52.9 us -> none  [shards(): old_of_new = jnp.zeros((unknowns,), jnp.int32).at[new_index].set(places)]
    select_n x5 -> x7, other arithmetic: 45.1 us -> 0.32 us  [the longest x5 0.25 us: rows_of(): return matrix.at[picks].get(mode='promise_in_bounds', unique_indices=True)]
    transpose x0 -> x4, local copies, waits for them, and re-layouts: none -> 33.9 us  [shards(): by_old = arrived.transpose(0, 2, 1).reshape(unknowns, width)]
  transfers between devices with their start and end apart: 2 -> 12, of which waited for: 2 -> 9; matrix products, arithmetic and copies ran while one was open for 5% -> 36% of each run, Pallas kernels for 0% -> 0%
where the time goes in v1:
time: 1160 us; the launch traced here: 1150 us
  waiting for transfers between devices  622 us (54%)
  local copies, waits for them, and re-layouts  385 us (33%)
  matrix products  63.6 us (5%)
  starting transfers between devices  38 us (3%)
  other arithmetic  31.5 us (3%)
  between operations  14 us (1%)
    all_to_all x4, waiting for transfers between devices, shards(): lax.all_to_all(outgoing, ('row', 'col'), split_axis=0, concat_axis=0, til...  521 us
    gather x8, local copies, waits for them, and re-layouts, rows_of(): return matrix.at[picks].get(mode='promise_in_bounds', unique_indices=True)  289 us
    all_to_all x4, waiting for transfers between devices, shards(): lax.all_to_all(chosen.transpose(0, 2, 1), 'col', split_axis=0, concat_axi...  75 us
    dot_general x4, matrix products, shards(): jnp.dot(moved.reshape(col_count * width, -1), check_vectors, precision=la...  62.5 us
    transpose x4, local copies, waits for them, and re-layouts, shards(): by_old = arrived.transpose(0, 2, 1).reshape(unknowns, width)  33.9 us
    reshape x4, local copies, waits for them, and re-layouts, shards(): rows_of(by_old, col_pick).reshape(col_count, unknowns // col_count, width)  33 us
    unnamed x3, local copies, waits for them, and re-layouts  28 us
    reduce_scatter x4, waiting for transfers between devices, shards(): lax.psum_scatter(partial, 'col', scatter_dimension=0, tiled=True)  25.9 us
  transfers between devices with their start and end apart: 12, of which 9 were waited for; matrix products, arithmetic and copies ran while one was open for 36% of the time, Pallas kernels for 0%

profile of v1, /device:TPU:0, one launch (start us, length us, event | category | flops | bytes accessed | tf_op | source)
XLA Modules:
  0.0 1153.5 jit_solution(1581270804039471345)
XLA Ops:
  7.2 28.0 %copy.11 = f32[448,14336]{0,1:T(8,128)} copy(f32[448,14336]{1,0:T(8,128)} %param.3) | data formatting | bytes 51380224 | tf_op args[0]
  35.3 9.2 select_convert_fusion.1
  45.9 20.9 %gather_fusion.6 = f32[3584,448]{1,0:T(8,128)} fusion(f32[14336,448]{1,0:T(8,128)} %bitcast.44, s32[4096]{0:T(1024)S(1)} %pad_clamp_fusion), kind=kCustom, calls=%fused_computation.6 | custom fusion | bytes 12859392 | tf_op jit(solution)/shard_map/gather | solution.py:34
  66.9 7.4 all-to-all-start.6
  74.5 21.0 %gather_fusion.4 = f32[3584,448]{1,0:T(8,128)} fusion(f32[14336,448]{1,0:T(8,128)} %bitcast.45, s32[4096]{0:T(1024)S(1)} %pad_clamp_fusion.1), kind=kCustom, calls=%fused_computation.4 | custom fusion | bytes 12859392 | tf_op jit(solution)/shard_map/gather | solution.py:34
  95.5 141.8 %all-to-all-done.6 = f32[32,112,448]{2,1,0:T(8,128)} async-done(((f32[32,112,448]{2,1,0:T(8,128)}), f32[32,112,448]{2,1,0:T(8,128)}, u32[]{:S(2)}, u32[]{:S(2)}) %all-to-all-start.6) | async-done | bytes 6422560 | tf_op jit(solution)/shard_map/all_to_all | solution.py:58
  241.1 20.9 %gather_fusion.2 = f32[3584,448]{1,0:T(8,128)} fusion(f32[14336,448]{1,0:T(8,128)} %bitcast.46, s32[4096]{0:T(1024)S(1)} %pad_clamp_fusion.2), kind=kCustom, calls=%fused_computation.2 | custom fusion | bytes 12859392 | tf_op jit(solution)/shard_map/gather | solution.py:34
  262.0 141.9 %all-to-all-done.4 = f32[32,112,448]{2,1,0:T(8,128)} async-done(((f32[32,112,448]{2,1,0:T(8,128)}), f32[32,112,448]{2,1,0:T(8,128)}, u32[]{:S(2)}, u32[]{:S(2)}) %all-to-all-start.4) | async-done | bytes 6422560 | tf_op jit(solution)/shard_map/all_to_all | solution.py:58
  407.8 21.1 %gather_fusion = f32[3584,448]{1,0:T(8,128)} fusion(f32[14336,448]{1,0:T(8,128)} %bitcast.47, s32[4096]{0:T(1024)S(1)} %pad_clamp_fusion.3), kind=kCustom, calls=%fused_computation | custom fusion | bytes 12859392 | tf_op jit(solution)/shard_map/gather | solution.py:34
  428.9 141.8 %all-to-all-done.2 = f32[32,112,448]{2,1,0:T(8,128)} async-done(((f32[32,112,448]{2,1,0:T(8,128)}), f32[32,112,448]{2,1,0:T(8,128)}, u32[]{:S(2)}, u32[]{:S(2)}) %all-to-all-start.2) | async-done | bytes 6422560 | tf_op jit(solution)/shard_map/all_to_all | solution.py:58
  574.5 8.4 copy.20
  582.9 51.0 %gather_fusion.7 = f32[14336,112]{1,0:T(8,128)} fusion(f32[14336,112]{1,0:T(8,128)} %bitcast.49, s32[14336]{0:T(1024)S(1)} %broadcast_clamp_fusion), kind=kCustom, calls=%fused_computation.7 | custom fusion | bytes 12902400 | tf_op jit(solution)/shard_map/gather | solution.py:34
  634.0 8.3 copy.21
  642.3 95.2 %all-to-all-done = f32[32,112,448]{2,1,0:T(8,128)} async-done(((f32[32,112,448]{2,1,0:T(8,128)}), f32[32,112,448]{2,1,0:T(8,128)}, u32[]{:S(2)}, u32[]{:S(2)}) %all-to-all-start) | async-done | bytes 6422560 | tf_op jit(solution)/shard_map/all_to_all | solution.py:58
  742.2 8.4 copy.18
  750.6 51.0 %gather_fusion.5 = f32[14336,112]{1,0:T(8,128)} fusion(f32[14336,112]{1,0:T(8,128)} %bitcast.50, s32[14336]{0:T(1024)S(1)} %broadcast_clamp_fusion), kind=kCustom, calls=%fused_computation.5 | custom fusion | bytes 12902400 | tf_op jit(solution)/shard_map/gather | solution.py:34
  801.6 8.2 copy.19
  809.8 5.3 all-to-all-done.7
  815.2 4.8 all-to-all-start.5
  820.2 15.6 %fusion.26 = f32[896,1024]{1,0:T(8,128)} fusion(f32[896,1792]{1,0:T(8,128)} %bitcast.30, f32[1792,1024]{1,0:T(8,128)} %param.5), kind=kOutput, calls=%fused_computation.62 | convolution fusion | flops 9865003008 | bytes 17432576 | tf_op jit(solution)/shard_map/dot_general | solution.py:63
  835.8 8.6 copy.16
  844.4 51.5 %gather_fusion.3 = f32[14336,112]{1,0:T(8,128)} fusion(f32[14336,112]{1,0:T(8,128)} %bitcast.51, s32[14336]{0:T(1024)S(1)} %broadcast_clamp_fusion), kind=kCustom, calls=%fused_computation.3 | custom fusion | bytes 12902400 | tf_op jit(solution)/shard_map/gather | solution.py:34
  895.9 8.3 copy.17
  909.4 15.6 %fusion.25 = f32[896,1024]{1,0:T(8,128)} fusion(f32[896,1792]{1,0:T(8,128)} %bitcast.29, f32[1792,1024]{1,0:T(8,128)} %param.5), kind=kOutput, calls=%fused_computation.61 | convolution fusion | flops 9865003008 | bytes 17432576 | tf_op jit(solution)/shard_map/dot_general | solution.py:63
  925.0 8.5 copy.13
  933.6 51.6 %gather_fusion.1 = f32[14336,112]{1,0:T(8,128)} fusion(f32[14336,112]{1,0:T(8,128)} %bitcast.48, s32[14336]{0:T(1024)S(1)} %broadcast_clamp_fusion), kind=kCustom, calls=%fused_computation.1 | custom fusion | bytes 12902400 | tf_op jit(solution)/shard_map/gather | solution.py:34
  985.1 8.2 copy.15
  999.0 15.6 %fusion.24 = f32[896,1024]{1,0:T(8,128)} fusion(f32[896,1792]{1,0:T(8,128)} %bitcast.28, f32[1792,1024]{1,0:T(8,128)} %param.5), kind=kOutput, calls=%fused_computation.60 | convolution fusion | flops 9865003008 | bytes 17432576 | tf_op jit(solution)/shard_map/dot_general | solution.py:63
  1014.6 68.7 %all-to-all-done.1 = f32[8,112,1792]{2,1,0:T(8,128)} async-done(((f32[8,112,1792]{2,1,0:T(8,128)}), f32[8,112,1792]{2,1,0:T(8,128)}, u32[]{:S(2)}, u32[]{:S(2)}) %all-to-all-start.1) | async-done | bytes 6422560 | tf_op jit(solution)/shard_map/all_to_all | solution.py:61
  1083.4 15.7 %fusion.23 = f32[896,1024]{1,0:T(8,128)} fusion(f32[896,1792]{1,0:T(8,128)} %bitcast.27, f32[1792,1024]{1,0:T(8,128)} %param.5), kind=kOutput, calls=%fused_computation.59 | convolution fusion | flops 9865003008 | bytes 17432576 | tf_op jit(solution)/shard_map/dot_general | solution.py:63
  1099.0 19.1 %pad_maximum_fusion = f32[8,448,1792]{2,1,0:T(8,128)} fusion(f32[8,112,1792]{2,1,0:T(8,128)} %all-to-all-done.7, f32[8,112,1792]{2,1,0:T(8,128)} %all-to-all-done.5, f32[8,112,1792]{2,1,0:T(8,128)} %all-to-all-done.3, f32[8,112,1792]{2,1,0:T(8,128)} %all-to-all-done.1), kind=kLoop, calls=%fused_computation.8 | loop fusion | flops 19267584 | bytes 51380224 | tf_op jit(solution)/shard_map/concatenate | solution.py:70
  1118.2 25.9 %reduce-scatter.5.cloned.1.call-done = f32[112,1024]{1,0:T(8,128)} async-done(((f32[896,1024]{1,0:T(8,128)}), f32[112,1024]{1,0:T(8,128)}) %reduce-scatter.5.cloned.1.call-update) | async-done | bytes 458768 | tf_op jit(solution)/shard_map/reduce_scatter | solution.py:69
  (46 shorter events, 31.8 us)
Async XLA Ops:
  7.2 28.0 %copy-start = (s32[14336]{0:T(1024)S(1)}, s32[14336]{0:T(1024)}, u32[]{:S(2)}) copy-start(s32[14336]{0:T(1024)} %param.4) | copy-start | bytes 172036
  66.9 170.4 %all-to-all-start.6 = ((f32[32,112,448]{2,1,0:T(8,128)}), f32[32,112,448]{2,1,0:T(8,128)}, u32[]{:S(2)}, u32[]{:S(2)}) async-start(f32[32,112,448]{2,1,0:T(8,128)} %bitcast.55), calls=%async_computation.6 | async-start | bytes 14680064 | tf_op jit(solution)/shard_map/all_to_all | solution.py:58
  237.3 166.7 %all-to-all-start.4 = ((f32[32,112,448]{2,1,0:T(8,128)}), f32[32,112,448]{2,1,0:T(8,128)}, u32[]{:S(2)}, u32[]{:S(2)}) async-start(f32[32,112,448]{2,1,0:T(8,128)} %bitcast.54), calls=%async_computation.4 | async-start | bytes 14680064 | tf_op jit(solution)/shard_map/all_to_all | solution.py:58
  404.0 166.7 %all-to-all-start.2 = ((f32[32,112,448]{2,1,0:T(8,128)}), f32[32,112,448]{2,1,0:T(8,128)}, u32[]{:S(2)}, u32[]{:S(2)}) async-start(f32[32,112,448]{2,1,0:T(8,128)} %bitcast.53), calls=%async_computation.2 | async-start | bytes 14680064 | tf_op jit(solution)/shard_map/all_to_all | solution.py:58
  570.7 166.7 %all-to-all-start = ((f32[32,112,448]{2,1,0:T(8,128)}), f32[32,112,448]{2,1,0:T(8,128)}, u32[]{:S(2)}, u32[]{:S(2)}) async-start(f32[32,112,448]{2,1,0:T(8,128)} %bitcast.52), calls=%async_computation | async-start | bytes 14680064 | tf_op jit(solution)/shard_map/all_to_all | solution.py:58
  737.4 77.7 %all-to-all-start.7 = ((f32[8,112,1792]{2,1,0:T(8,128)}), f32[8,112,1792]{2,1,0:T(8,128)}, u32[]{:S(2)}, u32[]{:S(2)}) async-start(f32[8,112,1792]{2,1,0:T(8,128)} %bitcast.64), calls=%async_computation.7 | async-start | bytes 12845056 | tf_op jit(solution)/shard_map/all_to_all | solution.py:61
  815.2 89.4 %all-to-all-start.5 = ((f32[8,112,1792]{2,1,0:T(8,128)}), f32[8,112,1792]{2,1,0:T(8,128)}, u32[]{:S(2)}, u32[]{:S(2)}) async-start(f32[8,112,1792]{2,1,0:T(8,128)} %bitcast.62), calls=%async_computation.5 | async-start | bytes 12845056 | tf_op jit(solution)/shard_map/all_to_all | solution.py:61
  819.9 298.2 %reduce-scatter.11.cloned.1.call-start = ((), (), s32[]{:S(2)}) async-start(), calls=%async_computation.15 | async-start | bytes 4128768 | tf_op jit(solution)/shard_map/reduce_scatter | solution.py:69
  904.5 89.4 %all-to-all-start.3 = ((f32[8,112,1792]{2,1,0:T(8,128)}), f32[8,112,1792]{2,1,0:T(8,128)}, u32[]{:S(2)}, u32[]{:S(2)}) async-start(f32[8,112,1792]{2,1,0:T(8,128)} %bitcast.61), calls=%async_computation.3 | async-start | bytes 12845056 | tf_op jit(solution)/shard_map/all_to_all | solution.py:61
  909.3 208.8 %reduce-scatter.9.cloned.1.call-start = ((), (), s32[]{:S(2)}) async-start(), calls=%async_computation.14 | async-start | bytes 4128768 | tf_op jit(solution)/shard_map/reduce_scatter | solution.py:69
  993.9 89.4 %all-to-all-start.1 = ((f32[8,112,1792]{2,1,0:T(8,128)}), f32[8,112,1792]{2,1,0:T(8,128)}, u32[]{:S(2)}, u32[]{:S(2)}) async-start(f32[8,112,1792]{2,1,0:T(8,128)} %bitcast.63), calls=%async_computation.1 | async-start | bytes 12845056 | tf_op jit(solution)/shard_map/all_to_all | solution.py:61
  998.7 119.5 %reduce-scatter.7.cloned.1.call-start = ((), (), s32[]{:S(2)}) async-start(), calls=%async_computation.13 | async-start | bytes 4128768 | tf_op jit(solution)/shard_map/reduce_scatter | solution.py:69
  1014.6 129.5 %reduce-scatter.5.cloned.1.call-start = ((), (), s32[]{:S(2)}) async-start(), calls=%async_computation.12 | async-start | bytes 4128768 | tf_op jit(solution)/shard_map/reduce_scatter | solution.py:69
Sparse Core Ops, SparseCore 0:
  835.9 72.7 reduce-scatter.10
  925.1 72.9 reduce-scatter.8
  1014.7 72.7 reduce-scatter.6
  1099.2 44.8 reduce-scatter.4

commit v2 on v1

--- a/solution.py
+++ b/solution.py
@@ -35,9 +35,19 @@
 
 
 def cuts_of(share):
-    step = -(-share // WIDTHS)
+    step = -(-2 * share // (2 * WIDTHS - 1))
     step = -(-step // 8) * 8
     return [(at, min(step, share - at)) for at in range(0, share, step)]
+
+
+def exchange(pieces, col, count):
+    held = jnp.zeros(pieces.shape, pieces.dtype)
+    for step in range(count):
+        piece = pieces[step]
+        if step:
+            piece = lax.ppermute(piece, "col", [(at, at ^ step) for at in range(count)])
+        held = lax.dynamic_update_slice(held, piece[None], (col ^ step, 0, 0))
+    return held
 
 
 def shards(normal_matrix, new_index, check_vectors):
@@ -47,28 +57,55 @@
     unknowns = new_index.shape[0]
     slab_rows = normal_matrix.shape[0]
     share = unknowns // devices
+    wide = unknowns // col_count
+    col = lax.axis_index("col")
     old_of_new = inverse_of(new_index)
     row_pick = cyclic(old_of_new, row_count).reshape(devices, share)
     col_pick = cyclic(old_of_new, col_count)
+    by_step = jnp.concatenate(
+        [lax.dynamic_slice(col_pick, ((col ^ step) * wide,), (wide,)) for step in range(col_count)]
+    )
     turned = normal_matrix.T
-    blocks, products = [], []
-    for at, width in cuts_of(share):
+    tile_layout = jnp.zeros((col_count, share, wide), normal_matrix.dtype)
+    partials, chosens, products = [], [], []
+    cuts = cuts_of(share)
+
+    def finish(chunk):
+        moved = exchange(chosens[chunk], col, col_count)
+        partials.append(
+            jnp.dot(
+                moved.reshape(-1, wide),
+                check_vectors,
+                precision=lax.Precision.HIGH,
+                preferred_element_type=jnp.float32,
+            )
+        )
+        return lax.dynamic_update_slice(tile_layout, moved, (0, cuts[chunk][0], 0))
+
+    def after(value, chunk):
+        held = ([chosens[chunk]] if chunk >= 0 else []) + ([partials[chunk - 1]] if chunk >= 1 else [])
+        if held:
+            value, *held = lax.optimization_barrier((value, *held))
+            if chunk >= 1:
+                partials[chunk - 1] = held.pop()
+            chosens[chunk] = held.pop()
+        return value
+
+    for chunk, (at, width) in enumerate(cuts):
         picks = row_pick[:, at : at + width].reshape(-1)
         outgoing = rows_of(turned, picks).reshape(devices, width, slab_rows)
+        outgoing = after(outgoing, chunk - 2)
         arrived = lax.all_to_all(outgoing, ("row", "col"), split_axis=0, concat_axis=0, tiled=True)
+        if chunk == len(cuts) - 1:
+            arrived = after(arrived, chunk - 1)
         by_old = arrived.transpose(0, 2, 1).reshape(unknowns, width)
-        chosen = rows_of(by_old, col_pick).reshape(col_count, unknowns // col_count, width)
-        moved = lax.all_to_all(chosen.transpose(0, 2, 1), "col", split_axis=0, concat_axis=0, tiled=True)
-        blocks.append(moved)
-        partial = jnp.dot(
-            moved.reshape(col_count * width, -1),
-            check_vectors,
-            precision=lax.Precision.HIGH,
-            preferred_element_type=jnp.float32,
-        )
-        products.append(lax.psum_scatter(partial, "col", scatter_dimension=0, tiled=True))
-    tile_layout = jnp.concatenate(blocks, axis=1).reshape(col_count * share, -1)
-    return (tile_layout, jnp.concatenate(products, axis=0))
+        picked = rows_of(by_old, by_step)
+        chosens.append(picked.reshape(col_count, wide, width).transpose(0, 2, 1))
+        if chunk >= 1:
+            tile_layout = finish(chunk - 1)
+    tile_layout = finish(len(cuts) - 1)
+    products = [lax.psum_scatter(part, "col", scatter_dimension=0, tiled=True) for part in partials]
+    return (tile_layout.reshape(col_count * share, wide), jnp.concatenate(products, axis=0))
 
 
 def solution(mesh):

time: 1160 us -> 1170 us (level)
  local copies, waits for them, and re-layouts: 385 us -> 504 us
  waiting for transfers between devices: 622 us -> 519 us
  other arithmetic: 31.5 us -> 13.1 us
  starting transfers between devices: 38 us -> 50.2 us
    all_to_all x4, waiting for transfers between devices: 521 us -> 203 us  [shards(): lax.all_to_all(outgoing, ('row', 'col'), split_axis=0, concat_axis=0, til...]
    ppermute x0 -> x28, waiting for transfers between devices: none -> 293 us  [exchange(): piece = lax.ppermute(piece, 'col', [(at, at ^ step) for at in range(count)])]
    all_to_all x4 -> x0, waiting for transfers between devices: 75 us -> none  [shards(): lax.all_to_all(chosen.transpose(0, 2, 1), 'col', split_axis=0, concat_axi...]
    dynamic_update_slice x0 -> x35, local copies, waits for them, and re-layouts: none -> 57.2 us  [the longest x4 29.2 us: finish(): return lax.dynamic_update_slice(tile_layout, moved, (0, cuts[chunk][0], 0))]
    broadcast_in_dim x0 -> x22, local copies, waits for them, and re-layouts: none -> 41.8 us  [the longest x21 41.5 us: exchange(): held = lax.dynamic_update_slice(held, piece[None], (col ^ step, 0, 0))]
    ppermute x0 -> x28, starting transfers between devices: none -> 31 us  [exchange(): piece = lax.ppermute(piece, 'col', [(at, at ^ step) for at in range(count)])]
    transpose x4 -> x1, local copies, waits for them, and re-layouts: 33.9 us -> 6.5 us  [shards(): by_old = arrived.transpose(0, 2, 1).reshape(unknowns, width)]
    concatenate x2 -> x1, other arithmetic: 21.9 us -> 2.88 us  [shards(): jnp.concatenate(products, axis=0)]
  transfers between devices with their start and end apart: 12 -> 36, of which waited for: 9 -> 16; matrix products, arithmetic and copies ran while one was open for 36% -> 43% of each run, Pallas kernels for 0% -> 0%
where the time goes in v2:
time: 1170 us; the launch traced here: 1160 us
  waiting for transfers between devices  519 us (44%)
  local copies, waits for them, and re-layouts  504 us (43%)
  matrix products  61.9 us (5%)
  starting transfers between devices  50.2 us (4%)
  between operations  14.6 us (1%)
  other arithmetic  13.1 us (1%)
    gather x8, local copies, waits for them, and re-layouts, rows_of(): return matrix.at[picks].get(mode='promise_in_bounds', unique_indices=True)  305 us
    ppermute x28, waiting for transfers between devices, exchange(): piece = lax.ppermute(piece, 'col', [(at, at ^ step) for at in range(count)])  293 us
    all_to_all x4, waiting for transfers between devices, shards(): lax.all_to_all(outgoing, ('row', 'col'), split_axis=0, concat_axis=0, til...  203 us
    dot_general x4, matrix products, finish(): jnp.dot(moved.reshape(-1, wide), check_vectors, precision=lax.Precision.H...  60.8 us
    broadcast_in_dim x21, local copies, waits for them, and re-layouts, exchange(): held = lax.dynamic_update_slice(held, piece[None], (col ^ step, 0, 0))  41.5 us
    ppermute x28, starting transfers between devices, exchange(): piece = lax.ppermute(piece, 'col', [(at, at ^ step) for at in range(count)])  31 us
    unnamed x44, local copies, waits for them, and re-layouts  30.4 us
    dynamic_update_slice x4, local copies, waits for them, and re-layouts, finish(): return lax.dynamic_update_slice(tile_layout, moved, (0, cuts[chunk][0], 0))  29.2 us
  transfers between devices with their start and end apart: 36, of which 16 were waited for; matrix products, arithmetic and copies ran while one was open for 43% of the time, Pallas kernels for 0%

profile of v2, /device:TPU:0, one launch (start us, length us, event | category | flops | bytes accessed | tf_op | source)
XLA Modules:
  0.0 1162.2 jit_solution(6210876142280111301)
XLA Ops:
  8.1 9.2 select_convert_fusion.1
  18.5 28.0 %copy.81 = f32[448,14336]{0,1:T(8,128)} copy(f32[448,14336]{1,0:T(8,128)} %param.3) | data formatting | bytes 51380224 | tf_op args[0]
  46.6 27.3 %gather_fusion = f32[4096,448]{1,0:T(8,128)} fusion(f32[14336,448]{1,0:T(8,128)} %bitcast.148, s32[4096]{0:T(1024)S(1)} %broadcast_clamp_fusion.3), kind=kCustom, calls=%fused_computation | custom fusion | bytes 14696448 | tf_op jit(solution)/shard_map/gather | solution.py:34
  73.8 8.7 copy.83
  90.0 27.3 %gather_fusion.2 = f32[4096,448]{1,0:T(8,128)} fusion(f32[14336,448]{1,0:T(8,128)} %bitcast.149, s32[4096]{0:T(1024)S(1)} %broadcast_clamp_fusion.2), kind=kCustom, calls=%fused_computation.2 | custom fusion | bytes 14696448 | tf_op jit(solution)/shard_map/gather | solution.py:34
  117.2 8.6 copy.93
  125.9 127.0 %all-to-all-done = f32[32,128,448]{1,2,0:T(8,128)} async-done(((f32[32,128,448]{1,2,0:T(8,128)}), f32[32,128,448]{1,2,0:T(8,128)}, u32[]{:S(2)}, u32[]{:S(2)}) %all-to-all-start) | async-done | bytes 7340064 | tf_op jit(solution)/shard_map/all_to_all | solution.py:98
  256.7 27.3 %gather_fusion.5 = f32[4096,448]{1,0:T(8,128)} fusion(f32[14336,448]{1,0:T(8,128)} %bitcast.150, s32[4096]{0:T(1024)S(1)} %broadcast_clamp_fusion.1), kind=kCustom, calls=%fused_computation.5 | custom fusion | bytes 14696448 | tf_op jit(solution)/shard_map/gather | solution.py:34
  284.3 51.0 %gather_fusion.1 = f32[14336,128]{1,0:T(8,128)} fusion(f32[14336,128]{1,0:T(8,128)} %bitcast.7, s32[14336]{0:T(1024)S(1)} %broadcast_clamp_fusion), kind=kCustom, calls=%fused_computation.1 | custom fusion | bytes 14737408 | tf_op jit(solution)/shard_map/gather | solution.py:34
  335.3 8.6 copy.102
  343.9 75.7 %all-to-all-done.1 = f32[32,128,448]{1,2,0:T(8,128)} async-done(((f32[32,128,448]{1,2,0:T(8,128)}), f32[32,128,448]{1,2,0:T(8,128)}, u32[]{:S(2)}, u32[]{:S(2)}) %all-to-all-start.1) | async-done | bytes 7340064 | tf_op jit(solution)/shard_map/all_to_all | solution.py:98
  435.2 82.4 %collective-permute-done.1 = f32[128,1792]{0,1:T(8,128)} collective-permute-done((f32[128,1792]{0,1:T(8,128)S(1)}, f32[128,1792]{0,1:T(8,128)}, u32[]{:S(2)}, u32[]{:S(2)}) %collective-permute-start.1) | collective-permute-done | bytes 917536 | tf_op jit(solution)/shard_map/ppermute | solution.py:48
  517.9 18.8 %gather_fusion.4 = f32[2048,448]{1,0:T(8,128)} fusion(f32[14336,448]{1,0:T(8,128)} %bitcast.151, s32[2048]{0:T(1024)S(1)} %broadcast_clamp_fusion.4), kind=kCustom, calls=%fused_computation.4 | custom fusion | bytes 7348224 | tf_op jit(solution)/shard_map/gather | solution.py:34
  537.0 51.4 %gather_fusion.3 = f32[14336,128]{1,0:T(8,128)} fusion(f32[14336,128]{1,0:T(8,128)} %bitcast.32, s32[14336]{0:T(1024)S(1)} %broadcast_clamp_fusion), kind=kCustom, calls=%fused_computation.3 | custom fusion | bytes 14737408 | tf_op jit(solution)/shard_map/gather | solution.py:34
  615.4 17.4 %fusion.20 = f32[1024,1024]{1,0:T(8,128)} fusion(f32[1024,1792]{1,0:T(8,128)} %bitcast.52, f32[1792,1024]{1,0:T(8,128)} %param.5), kind=kOutput, calls=%fused_computation.126 | convolution fusion | flops 11274289152 | bytes 18874368 | tf_op jit(solution)/shard_map/dot_general | solution.py:76
  648.2 50.3 %collective-permute-done.8 = f32[128,1792]{0,1:T(8,128)S(1)} collective-permute-done((f32[128,1792]{0,1:T(8,128)S(1)}, f32[128,1792]{0,1:T(8,128)S(1)}, u32[]{:S(2)}, u32[]{:S(2)}) %collective-permute-start.8) | collective-permute-done | bytes 917536 | tf_op jit(solution)/shard_map/ppermute | solution.py:48
  707.4 15.2 %collective-permute-done.9 = f32[128,1792]{0,1:T(8,128)} collective-permute-done((f32[128,1792]{0,1:T(8,128)S(1)}, f32[128,1792]{0,1:T(8,128)}, u32[]{:S(2)}, u32[]{:S(2)}) %collective-permute-start.9) | collective-permute-done | bytes 917536 | tf_op jit(solution)/shard_map/ppermute | solution.py:48
  728.8 15.9 %collective-permute-done.12 = f32[128,1792]{0,1:T(8,128)} collective-permute-done((f32[128,1792]{0,1:T(8,128)}, f32[128,1792]{0,1:T(8,128)}, u32[]{:S(2)}, u32[]{:S(2)}) %collective-permute-start.12) | collective-permute-done | bytes 917536 | tf_op jit(solution)/shard_map/ppermute | solution.py:48
  747.3 16.1 %collective-permute-done.13 = f32[128,1792]{0,1:T(8,128)} collective-permute-done((f32[128,1792]{0,1:T(8,128)}, f32[128,1792]{0,1:T(8,128)}, u32[]{:S(2)}, u32[]{:S(2)}) %collective-permute-start.13) | collective-permute-done | bytes 917536 | tf_op jit(solution)/shard_map/ppermute | solution.py:48
  774.3 18.4 %fusion.21 = f32[1024,1024]{1,0:T(8,128)} fusion(f32[1024,1792]{1,0:T(8,128)} %bitcast.60, f32[1792,1024]{1,0:T(8,128)} %param.5), kind=kOutput, calls=%fused_computation.127 | convolution fusion | flops 11274289152 | bytes 18874368 | tf_op jit(solution)/shard_map/dot_general | solution.py:76
  792.7 51.4 %gather_fusion.6 = f32[14336,128]{1,0:T(8,128)} fusion(f32[14336,128]{1,0:T(8,128)} %bitcast.57, s32[14336]{0:T(1024)S(1)} %broadcast_clamp_fusion), kind=kCustom, calls=%fused_computation.6 | custom fusion | bytes 14737408 | tf_op jit(solution)/shard_map/gather | solution.py:34
  850.6 51.0 %gather_fusion.7 = f32[14336,64]{1,0:T(8,128)} fusion(f32[14336,64]{1,0:T(8,128)} %bitcast.152, s32[14336]{0:T(1024)S(1)} %broadcast_clamp_fusion), kind=kCustom, calls=%fused_computation.7 | custom fusion | bytes 7397376 | tf_op jit(solution)/shard_map/gather | solution.py:34
  933.8 21.6 %collective-permute-done.25 = f32[64,1792]{1,0:T(8,128)S(1)} collective-permute-done((f32[64,1792]{1,0:T(8,128)S(1)}, f32[64,1792]{1,0:T(8,128)S(1)}, u32[]{:S(2)}, u32[]{:S(2)}) %collective-permute-start.25) | collective-permute-done | bytes 458784 | tf_op jit(solution)/shard_map/ppermute | solution.py:48
  957.5 7.5 fusion.23
  978.0 22.0 %collective-permute-done.15 = f32[128,1792]{0,1:T(8,128)S(1)} collective-permute-done((f32[128,1792]{0,1:T(8,128)S(1)}, f32[128,1792]{0,1:T(8,128)S(1)}, u32[]{:S(2)}, u32[]{:S(2)}) %collective-permute-start.15) | collective-permute-done | bytes 917536 | tf_op jit(solution)/shard_map/ppermute | solution.py:48
  1007.8 14.3 %collective-permute-done.16 = f32[128,1792]{0,1:T(8,128)} collective-permute-done((f32[128,1792]{0,1:T(8,128)S(1)}, f32[128,1792]{0,1:T(8,128)}, u32[]{:S(2)}, u32[]{:S(2)}) %collective-permute-start.16) | collective-permute-done | bytes 917536 | tf_op jit(solution)/shard_map/ppermute | solution.py:48
  1026.2 25.1 %collective-permute-done.18 = f32[128,1792]{0,1:T(8,128)} collective-permute-done((f32[128,1792]{0,1:T(8,128)}, f32[128,1792]{0,1:T(8,128)}, u32[]{:S(2)}, u32[]{:S(2)}) %collective-permute-start.18) | collective-permute-done | bytes 917536 | tf_op jit(solution)/shard_map/ppermute | solution.py:48
  1056.2 17.0 %collective-permute-done.20 = f32[128,1792]{0,1:T(8,128)} collective-permute-done((f32[128,1792]{0,1:T(8,128)}, f32[128,1792]{0,1:T(8,128)}, u32[]{:S(2)}, u32[]{:S(2)}) %collective-permute-start.20) | collective-permute-done | bytes 917536 | tf_op jit(solution)/shard_map/ppermute | solution.py:48
  1083.8 17.6 %fusion.22 = f32[1024,1024]{1,0:T(8,128)} fusion(f32[1024,1792]{1,0:T(8,128)} %bitcast.94, f32[1792,1024]{1,0:T(8,128)} %param.5), kind=kOutput, calls=%fused_computation.128 | convolution fusion | flops 11274289152 | bytes 18874368 | tf_op jit(solution)/shard_map/dot_general | solution.py:76
  1101.4 12.8 %dynamic_update_slice.116 = f32[8,448,1792]{2,1,0:T(8,128)} pad(f32[8,128,1792]{2,1,0:T(8,128)} %constant_dynamic-update-slice_fusion.27, f32[]{:T(128)} %constant.63.clone.1), padding=0_0x0_320x0_0 | pad | bytes 33030148 | tf_op jit(solution)/shard_map/dynamic_update_slice | solution.py:83
  1121.0 7.4 constant_dynamic-update-slice_fusion.9
  1130.6 21.9 %reduce-scatter.9.cloned.1.call-done = f32[128,1024]{1,0:T(8,128)} async-done(((f32[1024,1024]{1,0:T(8,128)}), f32[128,1024]{1,0:T(8,128)}) %reduce-scatter.9.cloned.1.call-update) | async-done | bytes 524304 | tf_op jit(solution)/shard_map/reduce_scatter | solution.py:107
  (199 shorter events, 193.3 us)
Async XLA Ops:
  82.5 170.4 %all-to-all-start = ((f32[32,128,448]{1,2,0:T(8,128)}), f32[32,128,448]{1,2,0:T(8,128)}, u32[]{:S(2)}, u32[]{:S(2)}) async-start(f32[32,128,448]{1,2,0:T(8,128)} %copy.83), calls=%async_computation | async-start | bytes 14680064 | tf_op jit(solution)/shard_map/all_to_all | solution.py:98
  252.9 166.7 %all-to-all-start.1 = ((f32[32,128,448]{1,2,0:T(8,128)}), f32[32,128,448]{1,2,0:T(8,128)}, u32[]{:S(2)}, u32[]{:S(2)}) async-start(f32[32,128,448]{1,2,0:T(8,128)} %copy.93), calls=%async_computation.1 | async-start | bytes 14680064 | tf_op jit(solution)/shard_map/all_to_all | solution.py:98
  419.6 213.2 %all-to-all-start.3 = ((f32[32,128,448]{1,2,0:T(8,128)}), f32[32,128,448]{1,2,0:T(8,128)}, u32[]{:S(2)}, u32[]{:S(2)}) async-start(f32[32,128,448]{1,2,0:T(8,128)} %copy.102), calls=%async_computation.3 | async-start | bytes 14680064 | tf_op jit(solution)/shard_map/all_to_all | solution.py:98
  429.0 88.6 %collective-permute-start.1 = (f32[128,1792]{0,1:T(8,128)S(1)}, f32[128,1792]{0,1:T(8,128)}, u32[]{:S(2)}, u32[]{:S(2)}) collective-permute-start(f32[128,1792]{0,1:T(8,128)S(1)} %get-tuple-element.35), channel_id=1, source_target_pairs={{0,2},{1,3},{2,0},{3,1},{4,6},{5,7},{6,4},{7,5},{8,10},{9,11},{10,... | collective-permute-start | bytes 2752520 | tf_op jit(solution)/shard_map/ppermute | solution.py:48
  430.8 165.1 %collective-permute-start.2 = (f32[128,1792]{0,1:T(8,128)S(1)}, f32[128,1792]{0,1:T(8,128)}, u32[]{:S(2)}, u32[]{:S(2)}) collective-permute-start(f32[128,1792]{0,1:T(8,128)S(1)} %get-tuple-element.34), channel_id=1, source_target_pairs={{0,3},{1,2},{2,1},{3,0},{4,7},{5,6},{6,5},{7,4},{8,11},{9,10},{10,... | collective-permute-start | bytes 2752520 | tf_op jit(solution)/shard_map/ppermute | solution.py:48
  430.8 166.6 %collective-permute-start.3 = (f32[128,1792]{0,1:T(8,128)}, f32[128,1792]{0,1:T(8,128)}, u32[]{:S(2)}, u32[]{:S(2)}) collective-permute-start(f32[128,1792]{0,1:T(8,128)} %get-tuple-element.33), channel_id=1, source_target_pairs={{0,4},{1,5},{2,6},{3,7},{4,0},{5,1},{6,2},{7,3},{8,12},{9,13},{10,... | collective-permute-start | bytes 2752520 | tf_op jit(solution)/shard_map/ppermute | solution.py:48
  432.6 167.3 %collective-permute-start.4 = (f32[128,1792]{0,1:T(8,128)}, f32[128,1792]{0,1:T(8,128)}, u32[]{:S(2)}, u32[]{:S(2)}) collective-permute-start(f32[128,1792]{0,1:T(8,128)} %get-tuple-element.32), channel_id=1, source_target_pairs={{0,5},{1,4},{2,7},{3,6},{4,1},{5,0},{6,3},{7,2},{8,13},{9,12},{10,... | collective-permute-start | bytes 2752520 | tf_op jit(solution)/shard_map/ppermute | solution.py:48
  432.6 169.6 %collective-permute-start.5 = (f32[128,1792]{0,1:T(8,128)}, f32[128,1792]{0,1:T(8,128)}, u32[]{:S(2)}, u32[]{:S(2)}) collective-permute-start(f32[128,1792]{0,1:T(8,128)} %get-tuple-element.31), channel_id=1, source_target_pairs={{0,6},{1,7},{2,4},{3,5},{4,2},{5,3},{6,0},{7,1},{8,14},{9,15},{10,... | collective-permute-start | bytes 2752520 | tf_op jit(solution)/shard_map/ppermute | solution.py:48
  517.6 87.2 %collective-permute-start.6 = (f32[128,1792]{0,1:T(8,128)}, f32[128,1792]{0,1:T(8,128)}, u32[]{:S(2)}, u32[]{:S(2)}) collective-permute-start(f32[128,1792]{0,1:T(8,128)} %get-tuple-element.30), channel_id=1, source_target_pairs={{0,7},{1,6},{2,5},{3,4},{4,3},{5,2},{6,1},{7,0},{8,15},{9,14},{10,... | collective-permute-start | bytes 2752520 | tf_op jit(solution)/shard_map/ppermute | solution.py:48
  632.7 211.3 %all-to-all-start.2 = ((f32[32,64,448]{2,1,0:T(8,128)}), f32[32,64,448]{2,1,0:T(8,128)}, u32[]{:S(2)}, u32[]{:S(2)}) async-start(f32[32,64,448]{2,1,0:T(8,128)} %bitcast.160), calls=%async_computation.2 | async-start | bytes 8388608 | tf_op jit(solution)/shard_map/all_to_all | solution.py:98
  636.3 494.3 %reduce-scatter.5.cloned.1.call-start = ((), (), s32[]{:S(2)}) async-start(), calls=%async_computation.8 | async-start | bytes 4718592 | tf_op jit(solution)/shard_map/reduce_scatter | solution.py:107
  643.6 54.9 %collective-permute-start.8 = (f32[128,1792]{0,1:T(8,128)S(1)}, f32[128,1792]{0,1:T(8,128)S(1)}, u32[]{:S(2)}, u32[]{:S(2)}) collective-permute-start(f32[128,1792]{0,1:T(8,128)S(1)} %get-tuple-element.27), channel_id=1, source_target_pairs={{0,2},{1,3},{2,0},{3,1},{4,6},{5,7},{6,4},{7,5},{8,10},{9,11},{10,... | collective-permute-start | bytes 2752520 | tf_op jit(solution)/shard_map/ppermute | solution.py:48
  643.8 78.7 %collective-permute-start.9 = (f32[128,1792]{0,1:T(8,128)S(1)}, f32[128,1792]{0,1:T(8,128)}, u32[]{:S(2)}, u32[]{:S(2)}) collective-permute-start(f32[128,1792]{0,1:T(8,128)S(1)} %get-tuple-element.26), channel_id=1, source_target_pairs={{0,3},{1,2},{2,1},{3,0},{4,7},{5,6},{6,5},{7,4},{8,11},{9,10},{10,... | collective-permute-start | bytes 2752520 | tf_op jit(solution)/shard_map/ppermute | solution.py:48
  645.0 79.0 %collective-permute-start.10 = (f32[128,1792]{0,1:T(8,128)}, f32[128,1792]{0,1:T(8,128)}, u32[]{:S(2)}, u32[]{:S(2)}) collective-permute-start(f32[128,1792]{0,1:T(8,128)} %get-tuple-element.25), channel_id=1, source_target_pairs={{0,4},{1,5},{2,6},{3,7},{4,0},{5,1},{6,2},{7,3},{8,12},{9,13},{10,... | collective-permute-start | bytes 2752520 | tf_op jit(solution)/shard_map/ppermute | solution.py:48
  645.5 80.9 %collective-permute-start.11 = (f32[128,1792]{0,1:T(8,128)}, f32[128,1792]{0,1:T(8,128)}, u32[]{:S(2)}, u32[]{:S(2)}) collective-permute-start(f32[128,1792]{0,1:T(8,128)} %get-tuple-element.24), channel_id=1, source_target_pairs={{0,5},{1,4},{2,7},{3,6},{4,1},{5,0},{6,3},{7,2},{8,13},{9,12},{10,... | collective-permute-start | bytes 2752520 | tf_op jit(solution)/shard_map/ppermute | solution.py:48
  647.1 97.6 %collective-permute-start.12 = (f32[128,1792]{0,1:T(8,128)}, f32[128,1792]{0,1:T(8,128)}, u32[]{:S(2)}, u32[]{:S(2)}) collective-permute-start(f32[128,1792]{0,1:T(8,128)} %get-tuple-element.23), channel_id=1, source_target_pairs={{0,6},{1,7},{2,4},{3,5},{4,2},{5,3},{6,0},{7,1},{8,14},{9,15},{10,... | collective-permute-start | bytes 2752520 | tf_op jit(solution)/shard_map/ppermute | solution.py:48
  698.5 64.9 %collective-permute-start.13 = (f32[128,1792]{0,1:T(8,128)}, f32[128,1792]{0,1:T(8,128)}, u32[]{:S(2)}, u32[]{:S(2)}) collective-permute-start(f32[128,1792]{0,1:T(8,128)} %get-tuple-element.22), channel_id=1, source_target_pairs={{0,7},{1,6},{2,5},{3,4},{4,3},{5,2},{6,1},{7,0},{8,15},{9,14},{10,... | collective-permute-start | bytes 2752520 | tf_op jit(solution)/shard_map/ppermute | solution.py:48
  765.8 364.8 %reduce-scatter.11.cloned.1.call-start = ((), (), s32[]{:S(2)}) async-start(), calls=%async_computation.11 | async-start | bytes 2359296 | tf_op jit(solution)/shard_map/reduce_scatter | solution.py:107
  912.0 13.4 %collective-permute-start.22 = (f32[64,1792]{1,0:T(8,128)S(1)}, f32[64,1792]{1,0:T(8,128)S(1)}, u32[]{:S(2)}, u32[]{:S(2)}) collective-permute-start(f32[64,1792]{1,0:T(8,128)S(1)} %get-tuple-element.43), channel_id=1, source_target_pairs={{0,2},{1,3},{2,0},{3,1},{4,6},{5,7},{6,4},{7,5},{8,10},{9,11},{10,... | collective-permute-start | bytes 1376264 | tf_op jit(solution)/shard_map/ppermute | solution.py:48
  913.0 20.7 %collective-permute-start.23 = (f32[64,1792]{1,0:T(8,128)S(1)}, f32[64,1792]{1,0:T(8,128)S(1)}, u32[]{:S(2)}, u32[]{:S(2)}) collective-permute-start(f32[64,1792]{1,0:T(8,128)S(1)} %get-tuple-element.42), channel_id=1, source_target_pairs={{0,3},{1,2},{2,1},{3,0},{4,7},{5,6},{6,5},{7,4},{8,11},{9,10},{10,... | collective-permute-start | bytes 1376264 | tf_op jit(solution)/shard_map/ppermute | solution.py:48
  913.4 20.4 %collective-permute-start.24 = (f32[64,1792]{1,0:T(8,128)S(1)}, f32[64,1792]{1,0:T(8,128)S(1)}, u32[]{:S(2)}, u32[]{:S(2)}) collective-permute-start(f32[64,1792]{1,0:T(8,128)S(1)} %get-tuple-element.41), channel_id=1, source_target_pairs={{0,4},{1,5},{2,6},{3,7},{4,0},{5,1},{6,2},{7,3},{8,12},{9,13},{10,... | collective-permute-start | bytes 1376264 | tf_op jit(solution)/shard_map/ppermute | solution.py:48
  915.8 39.6 %collective-permute-start.25 = (f32[64,1792]{1,0:T(8,128)S(1)}, f32[64,1792]{1,0:T(8,128)S(1)}, u32[]{:S(2)}, u32[]{:S(2)}) collective-permute-start(f32[64,1792]{1,0:T(8,128)S(1)} %get-tuple-element.40), channel_id=1, source_target_pairs={{0,5},{1,4},{2,7},{3,6},{4,1},{5,0},{6,3},{7,2},{8,13},{9,12},{10,... | collective-permute-start | bytes 1376264 | tf_op jit(solution)/shard_map/ppermute | solution.py:48
  915.8 39.6 %collective-permute-start.26 = (f32[64,1792]{1,0:T(8,128)S(1)}, f32[64,1792]{1,0:T(8,128)S(1)}, u32[]{:S(2)}, u32[]{:S(2)}) collective-permute-start(f32[64,1792]{1,0:T(8,128)S(1)} %get-tuple-element.39), channel_id=1, source_target_pairs={{0,6},{1,7},{2,4},{3,5},{4,2},{5,3},{6,0},{7,1},{8,14},{9,15},{10,... | collective-permute-start | bytes 1376264 | tf_op jit(solution)/shard_map/ppermute | solution.py:48
  925.4 30.3 %collective-permute-start.27 = (f32[64,1792]{1,0:T(8,128)S(1)}, f32[64,1792]{1,0:T(8,128)S(1)}, u32[]{:S(2)}, u32[]{:S(2)}) collective-permute-start(f32[64,1792]{1,0:T(8,128)S(1)} %get-tuple-element.38), channel_id=1, source_target_pairs={{0,7},{1,6},{2,5},{3,4},{4,3},{5,2},{6,1},{7,0},{8,15},{9,14},{10,... | collective-permute-start | bytes 1376264 | tf_op jit(solution)/shard_map/ppermute | solution.py:48
  965.0 165.6 %reduce-scatter.7.cloned.1.call-start = ((), (), s32[]{:S(2)}) async-start(), calls=%async_computation.9 | async-start | bytes 4718592 | tf_op jit(solution)/shard_map/reduce_scatter | solution.py:107
  965.8 186.8 %reduce-scatter.9.cloned.1.call-start = ((), (), s32[]{:S(2)}) async-start(), calls=%async_computation.10 | async-start | bytes 4718592 | tf_op jit(solution)/shard_map/reduce_scatter | solution.py:107
  971.4 28.6 %collective-permute-start.15 = (f32[128,1792]{0,1:T(8,128)S(1)}, f32[128,1792]{0,1:T(8,128)S(1)}, u32[]{:S(2)}, u32[]{:S(2)}) collective-permute-start(f32[128,1792]{0,1:T(8,128)S(1)} %get-tuple-element.19), channel_id=1, source_target_pairs={{0,2},{1,3},{2,0},{3,1},{4,6},{5,7},{6,4},{7,5},{8,10},{9,11},{10,... | collective-permute-start | bytes 2752520 | tf_op jit(solution)/shard_map/ppermute | solution.py:48
  973.3 48.8 %collective-permute-start.16 = (f32[128,1792]{0,1:T(8,128)S(1)}, f32[128,1792]{0,1:T(8,128)}, u32[]{:S(2)}, u32[]{:S(2)}) collective-permute-start(f32[128,1792]{0,1:T(8,128)S(1)} %get-tuple-element.18), channel_id=1, source_target_pairs={{0,3},{1,2},{2,1},{3,0},{4,7},{5,6},{6,5},{7,4},{8,11},{9,10},{10,... | collective-permute-start | bytes 2752520 | tf_op jit(solution)/shard_map/ppermute | solution.py:48
  973.3 50.3 %collective-permute-start.17 = (f32[128,1792]{0,1:T(8,128)}, f32[128,1792]{0,1:T(8,128)}, u32[]{:S(2)}, u32[]{:S(2)}) collective-permute-start(f32[128,1792]{0,1:T(8,128)} %get-tuple-element.17), channel_id=1, source_target_pairs={{0,4},{1,5},{2,6},{3,7},{4,0},{5,1},{6,2},{7,3},{8,12},{9,13},{10,... | collective-permute-start | bytes 2752520 | tf_op jit(solution)/shard_map/ppermute | solution.py:48
  975.1 76.3 %collective-permute-start.18 = (f32[128,1792]{0,1:T(8,128)}, f32[128,1792]{0,1:T(8,128)}, u32[]{:S(2)}, u32[]{:S(2)}) collective-permute-start(f32[128,1792]{0,1:T(8,128)} %get-tuple-element.16), channel_id=1, source_target_pairs={{0,5},{1,4},{2,7},{3,6},{4,1},{5,0},{6,3},{7,2},{8,13},{9,12},{10,... | collective-permute-start | bytes 2752520 | tf_op jit(solution)/shard_map/ppermute | solution.py:48
  975.1 78.7 %collective-permute-start.19 = (f32[128,1792]{0,1:T(8,128)}, f32[128,1792]{0,1:T(8,128)}, u32[]{:S(2)}, u32[]{:S(2)}) collective-permute-start(f32[128,1792]{0,1:T(8,128)} %get-tuple-element.15), channel_id=1, source_target_pairs={{0,6},{1,7},{2,4},{3,5},{4,2},{5,3},{6,0},{7,1},{8,14},{9,15},{10,... | collective-permute-start | bytes 2752520 | tf_op jit(solution)/shard_map/ppermute | solution.py:48
  1000.0 73.2 %collective-permute-start.20 = (f32[128,1792]{0,1:T(8,128)}, f32[128,1792]{0,1:T(8,128)}, u32[]{:S(2)}, u32[]{:S(2)}) collective-permute-start(f32[128,1792]{0,1:T(8,128)} %get-tuple-element.14), channel_id=1, source_target_pairs={{0,7},{1,6},{2,5},{3,4},{4,3},{5,2},{6,1},{7,0},{8,15},{9,14},{10,... | collective-permute-start | bytes 2752520 | tf_op jit(solution)/shard_map/ppermute | solution.py:48
  (22 other events, 273.0 us)
Sparse Core Ops, SparseCore 0:
  765.9 52.5 reduce-scatter.4
  965.1 50.7 reduce-scatter.10
  1019.3 71.7 reduce-scatter.6
  1101.5 50.9 reduce-scatter.8
